TPU v7x, 256 devices: a whole 4x4x8 slice. The times are simulated.
256 devices in a mesh: grp: 64 (over y, z, core), sub: 4 (over x).
Axes of the slice: x: 4, y: 4, z: 8, core: 2. Of those that a mesh axis runs over, the one named last changes fastest.
Arguments:
- adj_next: float32 [64, 128, 128, 128], P('grp', 'sub'), may hold values from -4.5 to 4.5
- adj_later: float32 [64, 128, 128, 128], P('grp', 'sub'), may hold values from -2.25 to 2.25
- box_sizes: int32 [64, 2], replicated, may hold values from 64 to 128, as said below
- holder: int32 [64], replicated, may hold values from 0 to 63, as said below
- partner: int32 [64, 2, 4], replicated, may hold values from -1 to 255, as said below
Outputs:
- adj_now: float32 [64, 128, 128, 128], P('grp', 'sub')
- adj_earlier: float32 [64, 128, 128, 128], P('grp', 'sub')
Inputs may be any that keep to these rules, and one draw needn't show every extreme that they name: box_sizes[p] = (Lx, Ly) with 64 <= Lx <= 128 and 64 <= Ly <= 128; some partition has Lx = 128 and Ly = 128, some has Lx = 64, some has Ly = 64. holder names every slot exactly once. The joining is mutual: if partner[p, f, s] = q * 4 + t then partner[q, 1 - f, t] = p * 4 + s, and q differs from p. A face may be joined in part and walled in part; some faces are wholly walls. Over both faces, a partition has at most 3 segments joined to any one other partition, and some pair of partitions has exactly 3.
All inputs are finite; a program needn't handle non-finite values.
Results may differ from a plain program's by a relative error of at most 0.0003.
Values sent between devices are 32-bit elements; how exact they have to be, the bound alone decides.
A program may use at most 128 MiB of HBM per device.

v0:
```python
import jax
import jax.numpy as jnp
from jax import lax
from jax.sharding import PartitionSpec as P

time_step = 0.5
precise = lax.Precision.HIGHEST
stencil_rows = (
    (0, 0, -2, 2, 0, 0),
    (0, 2, -27, 27, -2, 0),
    (-2, 27, -270, 270, -27, 2),
    (2, -27, 270, -270, 27, -2),
    (0, -2, 27, -27, 2, 0),
    (0, 0, 2, -2, 0, 0),
)


def cosine_table(size_cells, length):
    mode_index = jnp.arange(size_cells, dtype=jnp.int32)[:, None]
    cell_index = jnp.arange(size_cells, dtype=jnp.int32)[None, :]
    extent = length.astype(jnp.float32)
    angles = (
        jnp.pi * mode_index.astype(jnp.float32) * (cell_index.astype(jnp.float32) + 0.5) / extent
    )
    scaling = jnp.sqrt(jnp.where(mode_index == 0, 1.0, 2.0).astype(jnp.float32) / extent)
    inside = (mode_index < length) & (cell_index < length)
    return jnp.where(inside, scaling * jnp.cos(angles), jnp.float32(0.0))


def update_factors(len_x, len_y, first_y, count_y, total_x, total_z):
    wave_x = jnp.arange(total_x, dtype=jnp.int32).astype(jnp.float32) / len_x.astype(jnp.float32)
    wave_y = (first_y + jnp.arange(count_y, dtype=jnp.int32)).astype(jnp.float32) / len_y.astype(
        jnp.float32
    )
    wave_z = jnp.arange(total_z, dtype=jnp.int32).astype(jnp.float32) / jnp.float32(total_z)
    angular = jnp.pi * jnp.sqrt(
        wave_x[:, None, None] ** 2 + wave_y[None, :, None] ** 2 + wave_z[None, None, :] ** 2
    )
    two_cos = 2.0 * jnp.cos(angular * time_step)
    source = time_step**2 * jnp.sinc(angular * (time_step / (2.0 * jnp.pi))) ** 2
    return (two_cos, source.astype(jnp.float32))


def plane_inverse(spectral, table_y, table_z):
    physical = jnp.einsum("ly,xlm->xym", table_y, spectral, precision=precise)
    return jnp.einsum("mz,xym->xyz", table_z, physical, precision=precise)


def coupling_terms(own_strips, other_strips):
    weights = jnp.transpose(jnp.asarray(stencil_rows, dtype=jnp.float32)) / 180.0
    low_terms = jnp.einsum(
        "ij,...jw->...iw", weights[3:6, 0:3], other_strips[..., 0, :, :, :], precision=precise
    ) + jnp.einsum(
        "ij,...jw->...iw", weights[3:6, 3:6], own_strips[..., 0, :, :, :], precision=precise
    )
    high_terms = jnp.einsum(
        "ij,...jw->...iw", weights[0:3, 0:3], own_strips[..., 1, :, :, :], precision=precise
    ) + jnp.einsum(
        "ij,...jw->...iw", weights[0:3, 3:6], other_strips[..., 1, :, :, :], precision=precise
    )
    return jnp.stack([low_terms, high_terms], axis=-4)


def to_segments(strip_rows, pieces):
    x_cells, row_count, z_cells = strip_rows.shape
    layered = strip_rows.reshape(x_cells, row_count, pieces, z_cells // pieces)
    return jnp.transpose(layered, (2, 1, 0, 3)).reshape(
        pieces, row_count, x_cells * (z_cells // pieces)
    )


def from_segments(values, x_cells):
    pieces, row_count, flat_width = values.shape
    layered = values.reshape(pieces, row_count, x_cells, flat_width // x_cells)
    return jnp.transpose(layered, (2, 1, 0, 3)).reshape(
        x_cells, row_count, pieces * (flat_width // x_cells)
    )


def local(adj_next, adj_later, box_sizes, holder, partner):
    part_count = holder.shape[0]
    seg_count = partner.shape[2]
    item_count = 2 * seg_count
    my_group = lax.axis_index("grp")
    my_column = lax.axis_index("sub")
    sub_count = lax.axis_size("sub")
    x_local = adj_next.shape[1]
    y_cells = adj_next.shape[2]
    z_cells = adj_next.shape[3]
    x_total = x_local * sub_count
    y_local = y_cells // sub_count
    seg_cells = z_cells // seg_count
    strip_width = x_local * seg_cells
    part_ids = jnp.arange(part_count, dtype=jnp.int32)
    my_part = jnp.sum(jnp.where(holder == my_group, part_ids, 0))
    len_x = box_sizes[my_part, 0]
    len_y = box_sizes[my_part, 1]
    table_x = cosine_table(x_total, len_x)
    table_y = cosine_table(y_cells, len_y)
    table_z = cosine_table(z_cells, jnp.int32(z_cells))
    face_table = jnp.concatenate(
        [table_y[:, 0:3], lax.dynamic_slice_in_dim(table_y, len_y - 3, 3, 1)], axis=1
    )
    two_cos, source = update_factors(len_x, len_y, my_column * y_local, y_local, x_total, z_cells)
    x_global = my_column * x_local + jnp.arange(x_local, dtype=jnp.int32)
    y_index = jnp.arange(y_cells, dtype=jnp.int32)
    inside = ((x_global[:, None, None] < len_x) & (y_index[None, :, None] < len_y)).astype(
        jnp.float32
    )
    link_ids = partner[my_part].reshape(item_count)
    is_wall = link_ids < 0
    safe_links = jnp.maximum(link_ids, 0)
    peer_part = safe_links // seg_count
    peer_seg = safe_links % seg_count
    peer_group = holder[peer_part]
    item_ids = jnp.arange(item_count, dtype=jnp.int32)
    peer_item = (1 - item_ids // seg_count) * seg_count + peer_seg
    x_limit = jnp.minimum(len_x, box_sizes[peer_part, 0])
    column_x = my_column * x_local + jnp.arange(strip_width, dtype=jnp.int32) // seg_cells
    joined = ((column_x[None, :] < x_limit[:, None]) & jnp.logical_not(is_wall)[:, None]).astype(
        jnp.float32
    )
    joined = joined.reshape(2, seg_count, 1, strip_width)

    def reverse_step(current, earlier):
        spectral = jnp.einsum("mz,xyz->xym", table_z, current[0], precision=precise)
        spectral = jnp.einsum("ly,xym->xlm", table_y, spectral, precision=precise)
        spectral = lax.all_to_all(spectral, "sub", split_axis=1, concat_axis=0, tiled=True)
        spectral = jnp.einsum("kx,xlm->klm", table_x, spectral, precision=precise)
        wave_part = jnp.einsum("kx,klm->xlm", table_x, two_cos * spectral, precision=precise)
        force_part = jnp.einsum("kx,klm->xlm", table_x, source * spectral, precision=precise)
        wave_part, force_part = (
            lax.all_to_all(wave_part, "sub", split_axis=0, concat_axis=1, tiled=True),
            lax.all_to_all(force_part, "sub", split_axis=0, concat_axis=1, tiled=True),
        )
        face_rows = plane_inverse(force_part, face_table, table_z)
        wave_part = plane_inverse(wave_part, table_y, table_z)
        low_rows = face_rows[:, 0:3, :]
        high_rows = face_rows[:, 3:6, :]
        own_strips = jnp.concatenate(
            [to_segments(low_rows, seg_count), to_segments(high_rows, seg_count)], axis=0
        )
        everyone = lax.all_gather(own_strips[None], "grp", axis=0, tiled=True)
        everyone = everyone.reshape(part_count * item_count, 3, strip_width)
        other_strips = everyone[peer_group * item_count + peer_item]
        coupled = coupling_terms(
            own_strips.reshape(2, seg_count, 3, strip_width),
            other_strips.reshape(2, seg_count, 3, strip_width),
        )
        coupled = coupled * joined
        result = wave_part - inside * earlier[0]
        result = result.at[:, 0:3, :].add(from_segments(coupled[0], x_local))
        window = lax.dynamic_slice_in_dim(result, len_y - 3, 3, 1)
        result = lax.dynamic_update_slice_in_dim(
            result, window + from_segments(coupled[1], x_local), len_y - 3, 1
        )
        return result[None]

    adj_now = reverse_step(adj_next, adj_later)
    adj_earlier = reverse_step(adj_now, adj_next)
    return (adj_now, adj_earlier)


def solution(mesh):
    return jax.shard_map(
        local,
        mesh=mesh,
        in_specs=(P("grp", "sub", None, None), P("grp", "sub", None, None), P(), P(), P()),
        out_specs=(P("grp", "sub", None, None), P("grp", "sub", None, None)),
        check_vma=False,
    )
```

profile of v0, /device:TPU:1, one launch (start us, length us, event | category | flops | bytes accessed | tf_op | source)
XLA Modules:
  0.0 377.0 jit_solution(16978702654708273522)
XLA Ops:
  13.1 3.8 %fusion.15 = f32[128,32,128]{2,0,1:T(8,128)S(1)} fusion(f32[1,32,128,128]{3,2,1,0:T(8,128)} %param.11, f32[128]{0:T(128)S(1)} %get-tuple-element.45, f32[128]{0:T(128)S(1)} %get-tuple-element.46, f32[128]{0:T(128)S(1)} %get-tuple-element.47, pred[128]{0:T(512)(128)(4,1)S(1)} %iota_compare_fusion.1), kind=kOutput, calls=%fused_computation.27 | convolution fusion | flops 805388288 | bytes 4195968 | tf_op jit(solution)/shard_map/mz,xyz->xym/dot_general | solution.py:126
  16.9 2.1 fusion.32
  20.9 5.0 %all-to-all-start = ((f32[32,128,128]{2,0,1:T(8,128)}), f32[32,128,128]{2,0,1:T(8,128)S(1)}, u32[]{:S(2)}, u32[]{:S(2)}) async-start(f32[32,128,128]{2,0,1:T(8,128)} %copy.159), calls=%async_computation | async-start | bytes 4194304 | tf_op jit(solution)/shard_map/all_to_all | solution.py:128
  27.2 23.2 %all-to-all-done = f32[32,128,128]{2,0,1:T(8,128)S(1)} async-done(((f32[32,128,128]{2,0,1:T(8,128)}), f32[32,128,128]{2,0,1:T(8,128)S(1)}, u32[]{:S(2)}, u32[]{:S(2)}) %all-to-all-start) | async-done | bytes 2097184 | tf_op jit(solution)/shard_map/all_to_all | solution.py:128
  50.6 2.2 fusion.91
  52.8 5.3 %fusion.22 = f32[128,32,128]{2,0,1:T(8,128)S(1)} fusion(f32[128,32,128]{2,0,1:T(8,128)S(1)} %fusion.91, f32[128]{0:T(128)S(1)} %multiply_multiply_fusion.5, f32[128,32]{0,1:T(8,128)S(1)} %broadcast_add_fusion, f32[]{:T(128)S(6)} %convert_element_type.81, f32[128]{0:T(128)S(1)} %get-tuple-element.46, f32[128]{0:T(128)S(1)} %get-tuple-element.47, ...), kind=kOutput, calls=%fused_computation.34 | convolution fusion | flops 825311232 | bytes 4212868 | tf_op jit(solution)/shard_map/kx,klm->xlm/dot_general | solution.py:131
  58.2 2.5 copy.169
  60.7 4.4 %all-to-all-start.2 = ((f32[128,32,128]{2,1,0:T(8,128)}), f32[128,32,128]{2,1,0:T(8,128)}, u32[]{:S(2)}, u32[]{:S(2)}) async-start(f32[128,32,128]{2,1,0:T(8,128)} %copy.169), calls=%async_computation.2 | async-start | bytes 4194304 | tf_op jit(solution)/shard_map/all_to_all | solution.py:134
  67.1 21.8 %all-to-all-done.2 = f32[128,32,128]{2,1,0:T(8,128)} async-done(((f32[128,32,128]{2,1,0:T(8,128)}), f32[128,32,128]{2,1,0:T(8,128)}, u32[]{:S(2)}, u32[]{:S(2)}) %all-to-all-start.2) | async-done | bytes 2097184 | tf_op jit(solution)/shard_map/all_to_all | solution.py:134
  93.7 10.1 %fusion.30 = f32[128,32,128]{2,0,1:T(8,128)S(1)} fusion(f32[128,32,128]{2,0,1:T(8,128)S(1)} %fusion.91, f32[128]{0:T(128)S(1)} %multiply_multiply_fusion.5, f32[128,32]{0,1:T(8,128)S(1)} %broadcast_add_fusion, f32[]{:T(128)S(6)} %convert_element_type.81, f32[128]{0:T(128)S(1)} %get-tuple-element.46, f32[128]{0:T(128)S(1)} %get-tuple-element.47, ...), kind=kOutput, calls=%fused_computation.47 | convolution fusion | flops 807485440 | bytes 4212868 | tf_op jit(solution)/shard_map/kx,klm->xlm/dot_general | solution.py:130
  103.8 2.5 copy.163
  106.4 3.7 all-to-all-start.1
  113.7 19.2 %all-to-all-done.1 = f32[128,32,128]{2,1,0:T(8,128)S(1)} async-done(((f32[128,32,128]{2,1,0:T(8,128)}), f32[128,32,128]{2,1,0:T(8,128)S(1)}, u32[]{:S(2)}, u32[]{:S(2)}) %all-to-all-start.1) | async-done | bytes 2097184 | tf_op jit(solution)/shard_map/all_to_all | solution.py:133
  134.1 3.6 fusion.71
  137.7 4.2 %fusion.10 = f32[32,128,128]{2,1,0:T(8,128)S(1)} fusion(f32[1,32,128,128]{3,2,1,0:T(8,128)S(1)} %copy-done.5, f32[32,128,128]{2,1,0:T(8,128)S(1)} %fusion.71, f32[32,128]{1,0:T(8,128)S(1)} %and_convert_fusion.1, f32[128]{0:T(128)S(1)} %get-tuple-element.45, f32[128]{0:T(128)S(1)} %get-tuple-element.46, f32[128]{0:T(128)S(1)} %get-tuple-element.47, ...), kind=kOutput, calls=%fused_computation.21 | convolution fusion | flops 806436864 | bytes 6309504 | tf_op jit(solution)/shard_map/mz,xym->xyz/dot_general | solution.py:46
  141.9 38.0 %all-gather.5.cloned.1.call-done = f32[512,3,1024]{2,0,1:T(8,128)} async-done(((f32[8,3,1024]{2,0,1:T(8,128)}), f32[512,3,1024]{2,0,1:T(8,128)}) %all-gather.5.cloned.1.call-update) | async-done | bytes 6291472 | tf_op jit(solution)/shard_map/all_gather | solution.py:143
  179.9 10.5 %copy.175 = f32[512,3,1024]{2,1,0:T(4,128)} copy(f32[512,3,1024]{2,0,1:T(8,128)} %all-gather.5.cloned.1.call-done) | data formatting | bytes 12582912 | tf_op jit(solution)/shard_map/all_gather | solution.py:143
  190.4 4.0 %gather_fusion.1 = f32[8,3,1024]{2,1,0:T(4,128)S(1)} fusion(f32[512,3,1024]{2,1,0:T(4,128)} %copy.175, s32[1024]{0:T(1024)S(1)} %pad_clamp_fusion), kind=kCustom, calls=%fused_computation.1 | custom fusion | bytes 196640 | tf_op jit(solution)/shard_map/gather | solution.py:145
  196.6 2.3 fusion.84
  199.0 3.4 convolution_bitcast_fusion
  202.3 2.4 copy.187
  204.7 29.8 %all_to_all.108 = f32[32,128,128]{2,0,1:T(8,128)S(1)} all-to-all(f32[32,128,128]{2,0,1:T(8,128)S(1)} %copy.187), channel_id=1, replica_groups=mesh['grp'=64,'sub'=4] {'sub'}, dimensions={1} | all-to-all | bytes 4194304 | tf_op jit(solution)/shard_map/all_to_all | solution.py:128
  234.8 2.2 fusion.89
  237.0 5.3 %fusion.18 = f32[128,32,128]{2,0,1:T(8,128)S(1)} fusion(f32[128,32,128]{2,0,1:T(8,128)S(1)} %fusion.89, f32[128]{0:T(128)S(1)} %multiply_multiply_fusion.5, f32[128,32]{0,1:T(8,128)S(1)} %broadcast_add_fusion, f32[]{:T(128)S(6)} %convert_element_type.81, f32[128]{0:T(128)S(1)} %get-tuple-element.46, f32[128]{0:T(128)S(1)} %get-tuple-element.47, ...), kind=kOutput, calls=%fused_computation.30 | convolution fusion | flops 825311232 | bytes 4212868 | tf_op jit(solution)/shard_map/kx,klm->xlm/dot_general | solution.py:131
  243.6 27.2 %all_to_all.109 = f32[128,32,128]{2,1,0:T(8,128)S(1)} all-to-all(f32[128,32,128]{2,1,0:T(8,128)S(1)} %copy.197), channel_id=1, replica_groups=mesh['grp'=64,'sub'=4] {'sub'}, dimensions={0} | all-to-all | bytes 4194304 | tf_op jit(solution)/shard_map/all_to_all | solution.py:134
  274.1 9.9 %fusion.20 = f32[128,32,128]{2,0,1:T(8,128)S(1)} fusion(f32[128,32,128]{2,0,1:T(8,128)S(1)} %fusion.89, f32[128]{0:T(128)S(1)} %multiply_multiply_fusion.5, f32[128,32]{0,1:T(8,128)S(1)} %broadcast_add_fusion, f32[]{:T(128)S(6)} %convert_element_type.81, f32[128]{0:T(128)S(1)} %get-tuple-element.46, f32[128]{0:T(128)S(1)} %get-tuple-element.47, ...), kind=kOutput, calls=%fused_computation.32 | convolution fusion | flops 807485440 | bytes 4212868 | tf_op jit(solution)/shard_map/kx,klm->xlm/dot_general | solution.py:130
  285.2 26.3 %all_to_all.110 = f32[128,32,128]{2,1,0:T(8,128)S(1)} all-to-all(f32[128,32,128]{2,1,0:T(8,128)S(1)} %copy.191), channel_id=1, replica_groups=mesh['grp'=64,'sub'=4] {'sub'}, dimensions={0} | all-to-all | bytes 4194304 | tf_op jit(solution)/shard_map/all_to_all | solution.py:133
  312.3 3.6 fusion.68
  315.9 4.3 %fusion.17 = f32[32,128,128]{2,1,0:T(8,128)S(1)} fusion(f32[1,32,128,128]{3,2,1,0:T(8,128)S(1)} %copy-done.3, f32[32,128,128]{2,1,0:T(8,128)S(1)} %fusion.68, f32[32,128]{1,0:T(8,128)S(1)} %and_convert_fusion.1, f32[128]{0:T(128)S(1)} %get-tuple-element.45, f32[128]{0:T(128)S(1)} %get-tuple-element.46, f32[128]{0:T(128)S(1)} %get-tuple-element.47, ...), kind=kOutput, calls=%fused_computation.29 | convolution fusion | flops 806436864 | bytes 6309504 | tf_op jit(solution)/shard_map/mz,xym->xyz/dot_general | solution.py:46
  320.2 31.8 %all-gather.7.cloned.1.call-done = f32[512,3,1024]{2,0,1:T(8,128)} async-done(((f32[8,3,1024]{2,0,1:T(8,128)}), f32[512,3,1024]{2,0,1:T(8,128)}) %all-gather.7.cloned.1.call-update) | async-done | bytes 6291472 | tf_op jit(solution)/shard_map/all_gather | solution.py:143
  352.0 10.5 %copy.203 = f32[512,3,1024]{2,1,0:T(4,128)} copy(f32[512,3,1024]{2,0,1:T(8,128)} %all-gather.7.cloned.1.call-done) | data formatting | bytes 12582912 | tf_op jit(solution)/shard_map/all_gather | solution.py:143
  362.5 4.0 %gather_fusion.3 = f32[8,3,1024]{2,1,0:T(4,128)S(1)} fusion(f32[512,3,1024]{2,1,0:T(4,128)} %copy.203, s32[1024]{0:T(1024)S(1)} %pad_clamp_fusion), kind=kCustom, calls=%fused_computation.3 | custom fusion | bytes 196640 | tf_op jit(solution)/shard_map/gather | solution.py:145
  (121 shorter events, 28.2 us)
Async XLA Ops:
  20.9 29.5 %all-to-all-start = ((f32[32,128,128]{2,0,1:T(8,128)}), f32[32,128,128]{2,0,1:T(8,128)S(1)}, u32[]{:S(2)}, u32[]{:S(2)}) async-start(f32[32,128,128]{2,0,1:T(8,128)} %copy.159), calls=%async_computation | async-start | bytes 4194304 | tf_op jit(solution)/shard_map/all_to_all | solution.py:128
  60.7 28.1 %all-to-all-start.2 = ((f32[128,32,128]{2,1,0:T(8,128)}), f32[128,32,128]{2,1,0:T(8,128)}, u32[]{:S(2)}, u32[]{:S(2)}) async-start(f32[128,32,128]{2,1,0:T(8,128)} %copy.169), calls=%async_computation.2 | async-start | bytes 4194304 | tf_op jit(solution)/shard_map/all_to_all | solution.py:134
  65.2 114.8 %all-gather.5.cloned.1.call-start = ((), (), s32[]{:S(2)}) async-start(), calls=%async_computation.6 | async-start | bytes 6389760 | tf_op jit(solution)/shard_map/all_gather | solution.py:143
  106.4 3.8 %copy-start.6 = (s32[64,2,4]{0,2,1:T(4,128)S(1)}, s32[64,2,4]{0,2,1:T(4,128)}, u32[]{:S(2)}) copy-start(s32[64,2,4]{0,2,1:T(4,128)} %param.15) | copy-start | bytes 6148
  106.4 4.5 %copy-start = (s32[64]{0:T(128)S(1)}, s32[64]{0:T(128)}, u32[]{:S(2)}) copy-start(s32[64]{0:T(128)} %param.14) | copy-start | bytes 772
  106.4 5.2 %copy-start.1 = (s32[64,2]{0,1:T(2,128)S(1)}, s32[64,2]{0,1:T(2,128)}, u32[]{:S(2)}) copy-start(s32[64,2]{0,1:T(2,128)} %param.13) | copy-start | bytes 1540
  106.4 26.5 %all-to-all-start.1 = ((f32[128,32,128]{2,1,0:T(8,128)}), f32[128,32,128]{2,1,0:T(8,128)S(1)}, u32[]{:S(2)}, u32[]{:S(2)}) async-start(f32[128,32,128]{2,1,0:T(8,128)} %copy.163), calls=%async_computation.1 | async-start | bytes 4194304 | tf_op jit(solution)/shard_map/all_to_all | solution.py:133
  110.1 241.8 %all-gather.7.cloned.1.call-start = ((), (), s32[]{:S(2)}) async-start(), calls=%async_computation.7 | async-start | bytes 6389760 | tf_op jit(solution)/shard_map/all_gather | solution.py:143
  132.8 0.7 copy-start.10
  132.8 0.9 copy-start.9
  134.1 3.6 copy-start.5
  141.9 52.6 %copy-start.8 = (f32[3,3,1]{1,0,2:T(4,128)S(1)}, f32[3,3,1]{1,0,2:T(4,128)}, u32[]{:S(2)}) copy-start(f32[3,3,1]{1,0,2:T(4,128)} %constant.231) | copy-start | bytes 112
  141.9 52.8 %copy-start.7 = (f32[3,3,1]{1,0,2:T(4,128)S(1)}, f32[3,3,1]{1,0,2:T(4,128)}, u32[]{:S(2)}) copy-start(f32[3,3,1]{1,0,2:T(4,128)} %constant.228) | copy-start | bytes 112
  196.6 2.4 copy-start.2
  312.3 3.6 copy-start.3
  368.6 1.3 copy-start.4
Sparse Core Ops, SparseCore 0:
  93.8 86.0 all-gather.4
  274.2 77.6 all-gather.6
where the time goes:
time: 382 us; the launch traced here: 377 us
  waiting for transfers between devices  134 us (35%)
  blocking collectives  83.4 us (22%)
  matrix products  67.9 us (18%)
  local copies, waits for them, and re-layouts  52.6 us (14%)
  between operations  19.5 us (5%)
  starting transfers between devices  13.5 us (4%)
  other arithmetic  6.25 us (2%)
    all_gather x2, waiting for transfers between devices, reverse_step(): everyone = lax.all_gather(own_strips[None], 'grp', axis=0, tiled=True)  69.8 us
    all_to_all x1, blocking collectives, reverse_step(): lax.all_to_all(spectral, 'sub', split_axis=1, concat_axis=0, tiled=True)  29.8 us
    all_to_all x1, blocking collectives, reverse_step(): lax.all_to_all(force_part, 'sub', split_axis=0, concat_axis=1, tiled=True)  27.2 us
    all_to_all x1, blocking collectives, reverse_step(): lax.all_to_all(wave_part, 'sub', split_axis=0, concat_axis=1, tiled=True)  26.3 us
    all_to_all x1, waiting for transfers between devices, reverse_step(): lax.all_to_all(spectral, 'sub', split_axis=1, concat_axis=0, tiled=True)  23.2 us
    all_to_all x1, waiting for transfers between devices, reverse_step(): lax.all_to_all(force_part, 'sub', split_axis=0, concat_axis=1, tiled=True)  21.8 us
    all_gather x2, local copies, waits for them, and re-layouts, reverse_step(): everyone = lax.all_gather(own_strips[None], 'grp', axis=0, tiled=True)  21 us
    dot_general x2, matrix products, reverse_step(): jnp.einsum('kx,klm->xlm', table_x, two_cos * spectral, precision=precise)  20 us
  transfers between devices with their start and end apart: 5, of which 5 were waited for; matrix products, arithmetic and copies ran while one was open for 12% of the time, Pallas kernels for 0%

commit v1 on v0

--- a/solution.py
+++ b/solution.py
@@ -140,7 +140,13 @@
         own_strips = jnp.concatenate(
             [to_segments(low_rows, seg_count), to_segments(high_rows, seg_count)], axis=0
         )
-        everyone = lax.all_gather(own_strips[None], "grp", axis=0, tiled=True)
+        in_array = own_strips[None]
+        everyone = jnp.concatenate(
+            lax.all_to_all(
+                jnp.stack([in_array for _ in range(lax.psum(1, "grp"))], axis=0), "grp", 0, 0
+            ),
+            0,
+        )
         everyone = everyone.reshape(part_count * item_count, 3, strip_width)
         other_strips = everyone[peer_group * item_count + peer_item]
         coupled = coupling_terms(

time: 382 us -> 576 us (1.51)
  waiting for transfers between devices: 134 us -> 342 us
  blocking collectives: 83.4 us -> 29.4 us
  starting transfers between devices: 13.5 us -> 47.2 us
  local copies, waits for them, and re-layouts: 52.6 us -> 70.6 us
  between operations: 19.5 us -> 6.06 us
    all_to_all x0 -> x2, waiting for transfers between devices: none -> 260 us  [reverse_step(): lax.all_to_all(jnp.stack([in_array for _ in range(lax.psum(1, 'grp'))], a...]
    all_gather x2 -> x0, waiting for transfers between devices: 69.8 us -> none  [reverse_step(): everyone = lax.all_gather(own_strips[None], 'grp', axis=0, tiled=True)]
    all_to_all x2 -> x0, blocking collectives: 53.5 us -> none  [the longest x1 27.2 us: reverse_step(): lax.all_to_all(force_part, 'sub', split_axis=0, concat_axis=1, tiled=True)]
    all_to_all x0 -> x2, starting transfers between devices: none -> 27.2 us  [reverse_step(): lax.all_to_all(jnp.stack([in_array for _ in range(lax.psum(1, 'grp'))], a...]
    another operation x4 -> x8, local copies, waits for them, and re-layouts: 0.58 us -> 23 us  [the longest x2 15.6 us: reverse_step(): everyone = everyone.reshape(part_count * item_count, 3, strip_width)]
    all_gather x2 -> x0, local copies, waits for them, and re-layouts: 21 us -> none  [reverse_step(): everyone = lax.all_gather(own_strips[None], 'grp', axis=0, tiled=True)]
    all_to_all x1 -> x2, waiting for transfers between devices: 19.2 us -> 37.6 us  [reverse_step(): lax.all_to_all(wave_part, 'sub', split_axis=0, concat_axis=1, tiled=True)]
    all_to_all x0 -> x2, local copies, waits for them, and re-layouts: none -> 7.11 us  [reverse_step(): lax.all_to_all(jnp.stack([in_array for _ in range(lax.psum(1, 'grp'))], a...]
  transfers between devices with their start and end apart: 5 -> 7, of which waited for: 5 -> 7; matrix products, arithmetic and copies ran while one was open for 12% -> 10% of each run, Pallas kernels for 0% -> 0%
where the time goes in v1:
time: 576 us; the launch traced here: 571 us
  waiting for transfers between devices  342 us (59%)
  local copies, waits for them, and re-layouts  70.6 us (12%)
  matrix products  70.4 us (12%)
  starting transfers between devices  47.2 us (8%)
  blocking collectives  29.4 us (5%)
  between operations  6.06 us (1%)
    all_to_all x2, waiting for transfers between devices, reverse_step(): lax.all_to_all(jnp.stack([in_array for _ in range(lax.psum(1, 'grp'))], a...  260 us
    all_to_all x2, waiting for transfers between devices, reverse_step(): lax.all_to_all(wave_part, 'sub', split_axis=0, concat_axis=1, tiled=True)  37.6 us
    all_to_all x1, blocking collectives, reverse_step(): lax.all_to_all(spectral, 'sub', split_axis=1, concat_axis=0, tiled=True)  29.4 us
    all_to_all x2, starting transfers between devices, reverse_step(): lax.all_to_all(jnp.stack([in_array for _ in range(lax.psum(1, 'grp'))], a...  27.2 us
    all_to_all x1, waiting for transfers between devices, reverse_step(): lax.all_to_all(spectral, 'sub', split_axis=1, concat_axis=0, tiled=True)  23.1 us
    dot_general x2, matrix products, reverse_step(): jnp.einsum('kx,klm->xlm', table_x, two_cos * spectral, precision=precise)  22.6 us
    all_to_all x2, waiting for transfers between devices, reverse_step(): lax.all_to_all(force_part, 'sub', split_axis=0, concat_axis=1, tiled=True)  21.6 us
    another operation x2, local copies, waits for them, and re-layouts, reverse_step(): everyone = everyone.reshape(part_count * item_count, 3, strip_width)  15.6 us
  transfers between devices with their start and end apart: 7, of which 7 were waited for; matrix products, arithmetic and copies ran while one was open for 10% of the time, Pallas kernels for 0%

profile of v1, /device:TPU:1, one launch (start us, length us, event | category | flops | bytes accessed | tf_op | source)
XLA Modules:
  0.0 571.0 jit_solution(10243723752337649956)
XLA Ops:
  6.4 3.8 fusion.15
  14.3 5.0 all-to-all-start
  20.7 23.1 %all-to-all-done = f32[32,128,128]{2,0,1:T(8,128)S(1)} async-done(((f32[32,128,128]{2,0,1:T(8,128)}), f32[32,128,128]{2,0,1:T(8,128)S(1)}, u32[]{:S(2)}, u32[]{:S(2)}) %all-to-all-start) | async-done | bytes 2097184 | tf_op jit(solution)/shard_map/all_to_all | solution.py:128
  47.5 5.3 fusion.22
  55.4 4.0 all-to-all-start.2
  59.4 11.3 %fusion.30 = f32[128,32,128]{2,0,1:T(8,128)S(1)} fusion(f32[128,32,128]{2,0,1:T(8,128)} %copy-done.7, f32[128]{0:T(128)S(1)} %multiply_multiply_fusion.5, f32[128,32]{0,1:T(8,128)S(1)} %broadcast_add_fusion, f32[]{:T(128)S(6)} %convert_element_type.81, f32[128]{0:T(128)S(1)} %get-tuple-element.46, f32[128]{0:T(128)S(1)} %get-tuple-element.47, ...), kind=kOutput, calls=%fused_computation.49 | convolution fusion | flops 807485440 | bytes 4212868 | tf_op jit(solution)/shard_map/kx,klm->xlm/dot_general | solution.py:130
  73.3 9.7 %all-to-all-done.2 = f32[128,32,128]{2,1,0:T(8,128)S(1)} async-done(((f32[128,32,128]{2,1,0:T(8,128)}), f32[128,32,128]{2,1,0:T(8,128)S(1)}, u32[]{:S(2)}, u32[]{:S(2)}) %all-to-all-start.2) | async-done | bytes 2097184 | tf_op jit(solution)/shard_map/all_to_all | solution.py:134
  84.3 3.6 all-to-all-start.1
  93.6 17.1 %all-to-all-done.1 = f32[128,32,128]{2,1,0:T(8,128)S(1)} async-done(((f32[128,32,128]{2,1,0:T(8,128)}), f32[128,32,128]{2,1,0:T(8,128)S(1)}, u32[]{:S(2)}, u32[]{:S(2)}) %all-to-all-start.1) | async-done | bytes 2097184 | tf_op jit(solution)/shard_map/all_to_all | solution.py:133
  110.7 3.4 stack.24
  114.1 18.6 %all-to-all-start.3 = ((f32[64,1,8,3,1024]{4,2,3,1,0:T(8,128)}), f32[64,1,8,3,1024]{4,2,3,1,0:T(8,128)}, u32[]{:S(2)}, u32[]{:S(2)}) async-start(f32[64,1,8,3,1024]{4,2,3,1,0:T(8,128)} %stack.24), calls=%async_computation.3 | async-start | bytes 12582912 | tf_op jit(solution)/shard_map/all_to_all | solution.py:145
  137.6 3.6 fusion.71
  141.2 4.2 fusion.10
  145.4 127.9 %all-to-all-done.3 = f32[64,1,8,3,1024]{4,2,3,1,0:T(8,128)} async-done(((f32[64,1,8,3,1024]{4,2,3,1,0:T(8,128)}), f32[64,1,8,3,1024]{4,2,3,1,0:T(8,128)}, u32[]{:S(2)}, u32[]{:S(2)}) %all-to-all-start.3) | async-done | bytes 6291488 | tf_op jit(solution)/shard_map/all_to_all | solution.py:145
  273.4 3.6 copy.276
  276.9 7.8 %copy.180 = f32[512,3,1024]{2,1,0:T(4,128)} copy(f32[512,3,1024]{2,0,1:T(8,128)S(1)} %bitcast.205) | data formatting | bytes 12582912 | tf_op jit(solution)/shard_map/reshape;reshape | solution.py:150
  284.7 4.0 gather_fusion.1
  299.0 29.4 %all_to_all.118 = f32[32,128,128]{2,0,1:T(8,128)S(1)} all-to-all(f32[32,128,128]{2,0,1:T(8,128)S(1)} %copy.192), channel_id=1, replica_groups=mesh['grp'=64,'sub'=4] {'sub'}, dimensions={1} | all-to-all | bytes 4194304 | tf_op jit(solution)/shard_map/all_to_all | solution.py:128
  332.2 5.3 fusion.18
  340.1 3.8 all-to-all-start.6
  343.9 11.3 %fusion.20 = f32[128,32,128]{2,0,1:T(8,128)S(1)} fusion(f32[128,32,128]{2,0,1:T(8,128)} %copy-done.6, f32[128]{0:T(128)S(1)} %multiply_multiply_fusion.5, f32[128,32]{0,1:T(8,128)S(1)} %broadcast_add_fusion, f32[]{:T(128)S(6)} %convert_element_type.81, f32[128]{0:T(128)S(1)} %get-tuple-element.46, f32[128]{0:T(128)S(1)} %get-tuple-element.47, ...), kind=kOutput, calls=%fused_computation.34 | convolution fusion | flops 807485440 | bytes 4212868 | tf_op jit(solution)/shard_map/kx,klm->xlm/dot_general | solution.py:130
  357.7 11.8 %all-to-all-done.6 = f32[128,32,128]{2,1,0:T(8,128)S(1)} async-done(((f32[128,32,128]{2,1,0:T(8,128)}), f32[128,32,128]{2,1,0:T(8,128)S(1)}, u32[]{:S(2)}, u32[]{:S(2)}) %all-to-all-start.6) | async-done | bytes 2097184 | tf_op jit(solution)/shard_map/all_to_all | solution.py:134
  370.9 3.6 all-to-all-start.5
  378.7 20.6 %all-to-all-done.5 = f32[128,32,128]{2,1,0:T(8,128)S(1)} async-done(((f32[128,32,128]{2,1,0:T(8,128)}), f32[128,32,128]{2,1,0:T(8,128)S(1)}, u32[]{:S(2)}, u32[]{:S(2)}) %all-to-all-start.5) | async-done | bytes 2097184 | tf_op jit(solution)/shard_map/all_to_all | solution.py:133
  399.3 3.4 stack.28
  402.7 8.6 %all-to-all-start.7 = ((f32[64,1,8,3,1024]{4,2,3,1,0:T(8,128)}), f32[64,1,8,3,1024]{4,2,3,1,0:T(8,128)}, u32[]{:S(2)}, u32[]{:S(2)}) async-start(f32[64,1,8,3,1024]{4,2,3,1,0:T(8,128)} %stack.28), calls=%async_computation.7 | async-start | bytes 12582912 | tf_op jit(solution)/shard_map/all_to_all | solution.py:145
  412.0 3.6 fusion.68
  415.7 4.2 fusion.17
  419.9 132.0 %all-to-all-done.7 = f32[64,1,8,3,1024]{4,2,3,1,0:T(8,128)} async-done(((f32[64,1,8,3,1024]{4,2,3,1,0:T(8,128)}), f32[64,1,8,3,1024]{4,2,3,1,0:T(8,128)}, u32[]{:S(2)}, u32[]{:S(2)}) %all-to-all-start.7) | async-done | bytes 6291488 | tf_op jit(solution)/shard_map/all_to_all | solution.py:145
  551.9 3.6 copy.275
  555.5 7.8 %copy.209 = f32[512,3,1024]{2,1,0:T(4,128)} copy(f32[512,3,1024]{2,0,1:T(8,128)S(1)} %bitcast.206) | data formatting | bytes 12582912 | tf_op jit(solution)/shard_map/reshape;reshape | solution.py:150
  563.3 4.0 gather_fusion.3
  (133 shorter events, 55.9 us)
Async XLA Ops:
  14.3 29.5 %all-to-all-start = ((f32[32,128,128]{2,0,1:T(8,128)}), f32[32,128,128]{2,0,1:T(8,128)S(1)}, u32[]{:S(2)}, u32[]{:S(2)}) async-start(f32[32,128,128]{2,0,1:T(8,128)} %copy.163), calls=%async_computation | async-start | bytes 4194304 | tf_op jit(solution)/shard_map/all_to_all | solution.py:128
  46.2 1.3 copy-start.7
  55.4 27.6 %all-to-all-start.2 = ((f32[128,32,128]{2,1,0:T(8,128)}), f32[128,32,128]{2,1,0:T(8,128)S(1)}, u32[]{:S(2)}, u32[]{:S(2)}) async-start(f32[128,32,128]{2,1,0:T(8,128)} %copy.173), calls=%async_computation.2 | async-start | bytes 4194304 | tf_op jit(solution)/shard_map/all_to_all | solution.py:134
  83.0 1.3 copy-start.4
  84.3 26.4 %all-to-all-start.1 = ((f32[128,32,128]{2,1,0:T(8,128)}), f32[128,32,128]{2,1,0:T(8,128)S(1)}, u32[]{:S(2)}, u32[]{:S(2)}) async-start(f32[128,32,128]{2,1,0:T(8,128)} %copy.167), calls=%async_computation.1 | async-start | bytes 4194304 | tf_op jit(solution)/shard_map/all_to_all | solution.py:133
  114.1 18.6 %copy-start.10 = (s32[64,2,4]{0,2,1:T(4,128)S(1)}, s32[64,2,4]{0,2,1:T(4,128)}, u32[]{:S(2)}) copy-start(s32[64,2,4]{0,2,1:T(4,128)} %param.15) | copy-start | bytes 6148
  114.1 19.4 %copy-start = (s32[64]{0:T(128)S(1)}, s32[64]{0:T(128)}, u32[]{:S(2)}) copy-start(s32[64]{0:T(128)} %param.14) | copy-start | bytes 772
  114.1 20.0 %copy-start.1 = (s32[64,2]{0,1:T(2,128)S(1)}, s32[64,2]{0,1:T(2,128)}, u32[]{:S(2)}) copy-start(s32[64,2]{0,1:T(2,128)} %param.13) | copy-start | bytes 1540
  114.1 159.3 %all-to-all-start.3 = ((f32[64,1,8,3,1024]{4,2,3,1,0:T(8,128)}), f32[64,1,8,3,1024]{4,2,3,1,0:T(8,128)}, u32[]{:S(2)}, u32[]{:S(2)}) async-start(f32[64,1,8,3,1024]{4,2,3,1,0:T(8,128)} %stack.24), calls=%async_computation.3 | async-start | bytes 12582912 | tf_op jit(solution)/shard_map/all_to_all | solution.py:145
  136.3 0.7 copy-start.14
  136.4 0.9 copy-start.13
  137.6 3.6 copy-start.9
  276.9 11.8 %copy-start.12 = (f32[3,3,1]{1,0,2:T(4,128)S(1)}, f32[3,3,1]{1,0,2:T(4,128)}, u32[]{:S(2)}) copy-start(f32[3,3,1]{1,0,2:T(4,128)} %constant.231) | copy-start | bytes 112
  276.9 12.1 %copy-start.11 = (f32[3,3,1]{1,0,2:T(4,128)S(1)}, f32[3,3,1]{1,0,2:T(4,128)}, u32[]{:S(2)}) copy-start(f32[3,3,1]{1,0,2:T(4,128)} %constant.228) | copy-start | bytes 112
  290.9 2.4 copy-start.2
  330.9 1.3 copy-start.6
  340.1 29.4 %all-to-all-start.6 = ((f32[128,32,128]{2,1,0:T(8,128)}), f32[128,32,128]{2,1,0:T(8,128)S(1)}, u32[]{:S(2)}, u32[]{:S(2)}) async-start(f32[128,32,128]{2,1,0:T(8,128)} %copy.202), calls=%async_computation.6 | async-start | bytes 4194304 | tf_op jit(solution)/shard_map/all_to_all | solution.py:134
  369.6 1.3 copy-start.5
  370.9 28.4 %all-to-all-start.5 = ((f32[128,32,128]{2,1,0:T(8,128)}), f32[128,32,128]{2,1,0:T(8,128)S(1)}, u32[]{:S(2)}, u32[]{:S(2)}) async-start(f32[128,32,128]{2,1,0:T(8,128)} %copy.196), calls=%async_computation.5 | async-start | bytes 4194304 | tf_op jit(solution)/shard_map/all_to_all | solution.py:133
  402.7 149.2 %all-to-all-start.7 = ((f32[64,1,8,3,1024]{4,2,3,1,0:T(8,128)}), f32[64,1,8,3,1024]{4,2,3,1,0:T(8,128)}, u32[]{:S(2)}, u32[]{:S(2)}) async-start(f32[64,1,8,3,1024]{4,2,3,1,0:T(8,128)} %stack.28), calls=%async_computation.7 | async-start | bytes 12582912 | tf_op jit(solution)/shard_map/all_to_all | solution.py:145
  412.0 3.6 copy-start.3
  569.4 1.3 copy-start.8
